TPU v7x, 256 devices: a whole 4x4x8 slice. The times are simulated.
256 devices in a mesh: row: 16 (over z_hi, y), col: 16 (over x, z_lo, core).
Axes of the slice: x: 4, y: 4, z: 8 (z_hi: 4, z_lo: 2; z = z_hi * 2 + z_lo), core: 2. Of those that a mesh axis runs over, the one named last changes fastest.
Arguments:
- positions: float32 [3, 32768], P(None, ('row', 'col')), may hold values from 0 to 1
- radii: float32 [32768], P(('row', 'col')), may hold values from 0.5 to 2
- right_side: float32 [32768, 256], P(('row', 'col')), may hold values from -60 to 60, as said below
Outputs:
- solution: float32 [32768, 256], P(('row', 'col'))
- residual: float32 [32768, 256], P(('row', 'col'))
Inputs may be any that keep to these rules, and one draw needn't show every extreme that they name: `right_side`: real values of varying scale.
All inputs are finite; a program needn't handle non-finite values.
Results may differ from a plain program's by a relative error of at most 0.0003.
Values sent between devices are 32-bit elements; how exact they have to be, the bound alone decides.
A program may use at most 64 MiB of HBM per device.

v0:
```python
import jax
import jax.numpy as jnp
from jax import lax
from jax.sharding import PartitionSpec as P

ITERS = 2


def kernel_product(row_points, col_points, values, kernel_scale, softening, limit):
    row_count = row_points.shape[1]
    col_count = col_points.shape[1]
    blocks = max(1, row_count * col_count // limit)
    while row_count % blocks:
        blocks = blocks - 1
    block_size = row_count // blocks
    grouped = row_points.reshape(3, blocks, block_size).transpose(1, 0, 2)

    def apply_block(row_block):
        first = row_block[0][:, None] - col_points[0][None, :]
        second = row_block[1][:, None] - col_points[1][None, :]
        third = row_block[2][:, None] - col_points[2][None, :]
        squared = first * first + second * second + third * third
        weights = lax.rsqrt(squared + softening) * kernel_scale
        return jnp.dot(
            weights, values, preferred_element_type=jnp.float32, precision=lax.Precision.HIGHEST
        )

    return lax.map(apply_block, grouped).reshape(row_count, values.shape[1])


def constants(total):
    kernel_scale = float(total) ** (-0.5)
    spacing = 0.25 * float(total) ** (-1.0 / 3.0)
    return (kernel_scale, spacing * spacing)


def squares(residual):
    return lax.psum(jnp.sum(residual * residual, axis=0), ("row", "col"))


def body(positions, radii, right_side):
    local_count = positions.shape[1]
    total = local_count * lax.axis_size("row") * lax.axis_size("col")
    kernel_scale, softening = constants(total)
    row_points = lax.all_gather(positions, "col", axis=1, tiled=True)
    col_points = lax.all_gather(positions, "row", axis=1, tiled=True)
    limit = 1 << 20
    solution = jnp.zeros_like(right_side)
    residual = right_side
    direction = right_side
    norm_now = squares(residual)
    for iteration in range(ITERS):
        col_values = lax.all_gather(direction, "row", axis=0, tiled=True)
        summed = lax.psum_scatter(
            kernel_product(row_points, col_points, col_values, kernel_scale, softening, limit),
            "col",
            scatter_dimension=0,
            tiled=True,
        )
        image_vec = direction / radii[:, None] + summed
        curvature = lax.psum(jnp.sum(direction * image_vec, axis=0), ("row", "col"))
        step_size = norm_now / curvature
        solution = solution + step_size * direction
        residual = residual - step_size * image_vec
        if iteration + 1 < ITERS:
            norm_next = squares(residual)
            direction = residual + norm_next / norm_now * direction
            norm_now = norm_next
    return (solution, residual)


def solution(mesh):
    return jax.shard_map(
        body,
        mesh=mesh,
        in_specs=(P(None, ("row", "col")), P(("row", "col")), P(("row", "col"), None)),
        out_specs=(P(("row", "col"), None), P(("row", "col"), None)),
        check_vma=False,
    )
```

profile of v0, /device:TPU:1, one launch (start us, length us, event | category | flops | bytes accessed | tf_op | source)
XLA Modules:
  0.0 550.6 jit_solution(2993443880854321543)
XLA Ops:
  7.2 0.0 all-gather.3.cloned.1.call-start
  7.2 0.7 all-gather.3.cloned.1.call-update
  7.9 0.0 reduce-scatter.3.cloned.1.call-start
  7.9 40.7 %all_gather.13 = f32[3,2048]{1,0:T(4,128)S(1)} all-gather(f32[3,128]{1,0:T(4,128)} %param.7), channel_id=1, replica_groups=mesh['row'=16,'col'=16] {'row'}, dimensions={1}, use_global_device_ids=true | all-gather | bytes 26112 | tf_op jit(solution)/shard_map/all_gather | solution.py:46
  48.7 28.0 %all_gather.12 = f32[3,2048]{1,0:T(4,128)S(1)} all-gather(f32[3,128]{1,0:T(4,128)} %param.7), channel_id=1, replica_groups=mesh['row'=16,'col'=16] {'col'}, dimensions={1}, use_global_device_ids=true | all-gather | bytes 26112 | tf_op jit(solution)/shard_map/all_gather | solution.py:45
  76.6 0.2 broadcast.19.clone
  76.8 25.9 %while.20 = (s32[]{:T(128)}, f32[4,512,256]{2,1,0:T(8,128)S(1)}, f32[4,3,512]{2,1,0:T(4,128)S(1)}, f32[3,2048]{1,0:T(4,128)S(1)}, f32[2048,256]{1,0:T(8,128)}, /*index=5*/s32[]{:T(128)}, s32[]{:T(128)}, s32[]{}, s32[]{}) while((s32[]{:T(128)}, f32[4,512,256]{2,1,0:T(8,128)S(1)}, f32[4,3,512]{2,1,0:T(4,128)S(1)}, f32[3,2048]{1,0:T(4,128)S(1)}, ...), condition=%wide.region_3.4_spmd, body=%wide.region_2.3_spmd.sunk | while | flops 3231711232 | bytes 2713733 | solution.py:28
  76.8 6.4 %fusion.71 = f32[4,512,256]{2,1,0:T(8,128)S(1)} fusion(f32[4,512,256]{2,1,0:T(8,128)S(1)} %get-tuple-element.194, s32[]{:T(128)} %get-tuple-element.193, f32[2048,256]{1,0:T(8,128)} %get-tuple-element.206, f32[2048]{0:T(1024)S(1)} %bitcast.63, f32[512]{0:T(512)S(1)} %bitcast.70, f32[2048]{0:T(1024)S(1)} %bitcast.64, f32[512]{0:T(512)S(1)} %bitcast.69, ...), kind=kOutput, calls=%fused_computation.21.clone.1 | convolution fusion | flops 3231711232 | bytes 2652164 | tf_op jit(solution)/shard_map/while/body/eval_jaxpr/dot_general | solution.py:24
  83.3 6.4 %fusion.71 = f32[4,512,256]{2,1,0:T(8,128)S(1)} fusion(f32[4,512,256]{2,1,0:T(8,128)S(1)} %get-tuple-element.194, s32[]{:T(128)} %get-tuple-element.193, f32[2048,256]{1,0:T(8,128)} %get-tuple-element.206, f32[2048]{0:T(1024)S(1)} %bitcast.63, f32[512]{0:T(512)S(1)} %bitcast.70, f32[2048]{0:T(1024)S(1)} %bitcast.64, f32[512]{0:T(512)S(1)} %bitcast.69, ...), kind=kOutput, calls=%fused_computation.21.clone.1 | convolution fusion | flops 3231711232 | bytes 2652164 | tf_op jit(solution)/shard_map/while/body/eval_jaxpr/dot_general | solution.py:24
  89.8 6.4 %fusion.71 = f32[4,512,256]{2,1,0:T(8,128)S(1)} fusion(f32[4,512,256]{2,1,0:T(8,128)S(1)} %get-tuple-element.194, s32[]{:T(128)} %get-tuple-element.193, f32[2048,256]{1,0:T(8,128)} %get-tuple-element.206, f32[2048]{0:T(1024)S(1)} %bitcast.63, f32[512]{0:T(512)S(1)} %bitcast.70, f32[2048]{0:T(1024)S(1)} %bitcast.64, f32[512]{0:T(512)S(1)} %bitcast.69, ...), kind=kOutput, calls=%fused_computation.21.clone.1 | convolution fusion | flops 3231711232 | bytes 2652164 | tf_op jit(solution)/shard_map/while/body/eval_jaxpr/dot_general | solution.py:24
  96.3 6.4 %fusion.71 = f32[4,512,256]{2,1,0:T(8,128)S(1)} fusion(f32[4,512,256]{2,1,0:T(8,128)S(1)} %get-tuple-element.194, s32[]{:T(128)} %get-tuple-element.193, f32[2048,256]{1,0:T(8,128)} %get-tuple-element.206, f32[2048]{0:T(1024)S(1)} %bitcast.63, f32[512]{0:T(512)S(1)} %bitcast.70, f32[2048]{0:T(1024)S(1)} %bitcast.64, f32[512]{0:T(512)S(1)} %bitcast.69, ...), kind=kOutput, calls=%fused_computation.21.clone.1 | convolution fusion | flops 3231711232 | bytes 2652164 | tf_op jit(solution)/shard_map/while/body/eval_jaxpr/dot_general | solution.py:24
  102.7 1.3 copy-done.1
  104.1 0.0 all-gather.5.cloned.1.call-start
  104.1 58.5 %reduce-scatter.3.cloned.1.call-done = f32[128,256]{1,0:T(8,128)} async-done(((f32[2048,256]{1,0:T(8,128)}), f32[128,256]{1,0:T(8,128)}) %reduce-scatter.3.cloned.1.call-update) | async-done | bytes 131088 | tf_op jit(solution)/shard_map/reduce_scatter | solution.py:54
  162.6 1.0 multiply_reduce_fusion.2
  163.6 79.5 %all-reduce = (f32[256]{0:T(256)S(1)}, f32[256]{0:T(256)S(1)}) all-reduce(f32[256]{0:T(256)S(1)} %get-tuple-element.59, f32[256]{0:T(256)S(1)} %get-tuple-element.58), channel_id=1, replica_groups=mesh['row'=16,'col'=16] {'row','col'}, use_global_device_ids=true, to_apply=%region_1.0 | all-reduce | flops 512 | bytes 4096 | tf_op jit(solution)/shard_map/psum | solution.py:38
  243.1 1.0 multiply_reduce_fusion.1
  244.1 72.5 %psum.30 = f32[256]{0:T(256)S(1)} all-reduce(f32[256]{0:T(256)S(1)} %get-tuple-element.82), channel_id=1, replica_groups=mesh['row'=16,'col'=16] {'row','col'}, use_global_device_ids=true, to_apply=%region_8.9 | all-reduce | flops 256 | bytes 2048 | tf_op jit(solution)/shard_map/psum | solution.py:38
  316.6 0.7 multiply_add_fusion.1
  317.3 0.2 reduce-scatter.5.cloned.1.call-start
  317.6 55.1 %all-gather.5.cloned.1.call-done = f32[2048,256]{1,0:T(8,128)} async-done(((f32[128,256]{1,0:T(8,128)}), f32[2048,256]{1,0:T(8,128)}) %all-gather.5.cloned.1.call-update) | async-done | bytes 2097168 | tf_op jit(solution)/shard_map/all_gather | solution.py:53
  372.7 0.2 broadcast.19
  372.9 25.9 %while.21 = (s32[]{:T(128)}, f32[4,512,256]{2,1,0:T(8,128)S(1)}, f32[4,3,512]{2,1,0:T(4,128)S(1)}, f32[3,2048]{1,0:T(4,128)S(1)}, f32[2048,256]{1,0:T(8,128)}, /*index=5*/s32[]{:T(128)}, s32[]{:T(128)}, s32[]{}, s32[]{}) while((s32[]{:T(128)}, f32[4,512,256]{2,1,0:T(8,128)S(1)}, f32[4,3,512]{2,1,0:T(4,128)S(1)}, f32[3,2048]{1,0:T(4,128)S(1)}, ...), condition=%wide.region_10.11_spmd, body=%wide.region_9.10_spmd.sunk | while | flops 3231711232 | bytes 2713733 | solution.py:28
  372.9 6.4 %fusion.75 = f32[4,512,256]{2,1,0:T(8,128)S(1)} fusion(f32[4,512,256]{2,1,0:T(8,128)S(1)} %get-tuple-element.221, s32[]{:T(128)} %get-tuple-element.220, f32[2048,256]{1,0:T(8,128)} %get-tuple-element.233, f32[2048]{0:T(1024)S(1)} %bitcast.66, f32[512]{0:T(512)S(1)} %bitcast.73, f32[2048]{0:T(1024)S(1)} %bitcast.67, f32[512]{0:T(512)S(1)} %bitcast.72, ...), kind=kOutput, calls=%fused_computation.48.clone.1 | convolution fusion | flops 3231711232 | bytes 2652164 | tf_op jit(solution)/shard_map/while/body/eval_jaxpr/dot_general | solution.py:24
  379.4 6.4 %fusion.75 = f32[4,512,256]{2,1,0:T(8,128)S(1)} fusion(f32[4,512,256]{2,1,0:T(8,128)S(1)} %get-tuple-element.221, s32[]{:T(128)} %get-tuple-element.220, f32[2048,256]{1,0:T(8,128)} %get-tuple-element.233, f32[2048]{0:T(1024)S(1)} %bitcast.66, f32[512]{0:T(512)S(1)} %bitcast.73, f32[2048]{0:T(1024)S(1)} %bitcast.67, f32[512]{0:T(512)S(1)} %bitcast.72, ...), kind=kOutput, calls=%fused_computation.48.clone.1 | convolution fusion | flops 3231711232 | bytes 2652164 | tf_op jit(solution)/shard_map/while/body/eval_jaxpr/dot_general | solution.py:24
  385.9 6.4 %fusion.75 = f32[4,512,256]{2,1,0:T(8,128)S(1)} fusion(f32[4,512,256]{2,1,0:T(8,128)S(1)} %get-tuple-element.221, s32[]{:T(128)} %get-tuple-element.220, f32[2048,256]{1,0:T(8,128)} %get-tuple-element.233, f32[2048]{0:T(1024)S(1)} %bitcast.66, f32[512]{0:T(512)S(1)} %bitcast.73, f32[2048]{0:T(1024)S(1)} %bitcast.67, f32[512]{0:T(512)S(1)} %bitcast.72, ...), kind=kOutput, calls=%fused_computation.48.clone.1 | convolution fusion | flops 3231711232 | bytes 2652164 | tf_op jit(solution)/shard_map/while/body/eval_jaxpr/dot_general | solution.py:24
  392.3 6.4 %fusion.75 = f32[4,512,256]{2,1,0:T(8,128)S(1)} fusion(f32[4,512,256]{2,1,0:T(8,128)S(1)} %get-tuple-element.221, s32[]{:T(128)} %get-tuple-element.220, f32[2048,256]{1,0:T(8,128)} %get-tuple-element.233, f32[2048]{0:T(1024)S(1)} %bitcast.66, f32[512]{0:T(512)S(1)} %bitcast.73, f32[2048]{0:T(1024)S(1)} %bitcast.67, f32[512]{0:T(512)S(1)} %bitcast.72, ...), kind=kOutput, calls=%fused_computation.48.clone.1 | convolution fusion | flops 3231711232 | bytes 2652164 | tf_op jit(solution)/shard_map/while/body/eval_jaxpr/dot_general | solution.py:24
  398.8 1.3 copy-done
  400.1 61.9 %reduce-scatter.5.cloned.1.call-done = f32[128,256]{1,0:T(8,128)} async-done(((f32[2048,256]{1,0:T(8,128)}), f32[128,256]{1,0:T(8,128)}) %reduce-scatter.5.cloned.1.call-update) | async-done | bytes 131088 | tf_op jit(solution)/shard_map/reduce_scatter | solution.py:54
  462.0 1.0 multiply_reduce_fusion
  463.0 79.4 %psum.31 = f32[256]{0:T(256)S(1)} all-reduce(f32[256]{0:T(256)S(1)} %multiply_reduce_fusion), channel_id=1, replica_groups=mesh['row'=16,'col'=16] {'row','col'}, use_global_device_ids=true, to_apply=%region_13.14 | all-reduce | flops 256 | bytes 2048 | tf_op jit(solution)/shard_map/psum | solution.py:61
  542.4 1.7 multiply_subtract_fusion
  (31 shorter events, 0.4 us)
Async XLA Ops:
  7.2 69.5 %all-gather.3.cloned.1.call-start = ((), (), s32[]{:S(2)}) async-start(), calls=%async_computation.2 | async-start | bytes 2228224 | tf_op jit(solution)/shard_map/all_gather | solution.py:53
  7.9 154.7 %reduce-scatter.3.cloned.1.call-start = ((), (), s32[]{:S(2)}) async-start(), calls=%async_computation.3 | async-start | bytes 2228224 | tf_op jit(solution)/shard_map/reduce_scatter | solution.py:54
  102.7 1.3 copy-start.1
  102.7 59.9 %copy-start.2 = (f32[128,256]{1,0:T(8,128)S(1)}, f32[128,256]{1,0:T(8,128)}, u32[]{:S(2)}) copy-start(f32[128,256]{1,0:T(8,128)} %param.9) | copy-start | bytes 393220
  102.7 59.9 %copy-start.4 = (f32[128]{0:T(128)S(1)}, f32[128]{0:T(128)}, u32[]{:S(2)}) copy-start(f32[128]{0:T(128)} %param.8) | copy-start | bytes 1540
  104.1 268.6 %all-gather.5.cloned.1.call-start = ((), (), s32[]{:S(2)}) async-start(), calls=%async_computation.4 | async-start | bytes 2228224 | tf_op jit(solution)/shard_map/all_gather | solution.py:53
  317.3 144.7 %reduce-scatter.5.cloned.1.call-start = ((), (), s32[]{:S(2)}) async-start(), calls=%async_computation.5 | async-start | bytes 2228224 | tf_op jit(solution)/shard_map/reduce_scatter | solution.py:54
  398.7 1.3 copy-start
  398.7 63.2 %copy-start.3 = (f32[128,256]{1,0:T(8,128)S(1)}, f32[128,256]{1,0:T(8,128)}, u32[]{:S(2)}) copy-start(f32[128,256]{1,0:T(8,128)} %multiply_add_fusion.1) | copy-start | bytes 393220
Sparse Core Ops, SparseCore 0:
  10.4 62.6 all-gather.2
  104.2 58.3 reduce-scatter.2
  317.4 55.2 all-gather.4
  400.2 61.7 reduce-scatter.4
where the time goes:
time: 551 us
  blocking collectives  300 us (54%)
  waiting for transfers between devices  176 us (32%)
  matrix products  51.2 us (9%)
  between operations  13.8 us (3%)
    psum x2, blocking collectives, squares(): return lax.psum(jnp.sum(residual * residual, axis=0), ('row', 'col'))  152 us
    reduce_scatter x2, waiting for transfers between devices, body(): lax.psum_scatter(kernel_product(row_points, col_points, col_values, kerne...  120 us
    psum x1, blocking collectives, body(): curvature = lax.psum(jnp.sum(direction * image_vec, axis=0), ('row', 'col'))  79.4 us
    all_gather x2, waiting for transfers between devices, body(): col_values = lax.all_gather(direction, 'row', axis=0, tiled=True)  55.1 us
    dot_general x8, matrix products, apply_block(): jnp.dot(weights, values, preferred_element_type=jnp.float32, precision=la...  51.2 us
    all_gather x1, blocking collectives, body(): col_points = lax.all_gather(positions, 'row', axis=1, tiled=True)  40.7 us
    all_gather x1, blocking collectives, body(): row_points = lax.all_gather(positions, 'col', axis=1, tiled=True)  28 us
  transfers between devices with their start and end apart: 4, of which 3 were waited for; matrix products, arithmetic and copies ran while one was open for 0% of the time, Pallas kernels for 0%

commit v1 on v0

--- a/solution.py
+++ b/solution.py
@@ -35,7 +35,7 @@
 
 
 def squares(residual):
-    return lax.psum(jnp.sum(residual * residual, axis=0), ("row", "col"))
+    return lax.psum(lax.psum(jnp.sum(residual * residual, axis=0), "col"), "row")
 
 
 def body(positions, radii, right_side):

time: 551 us -> 615 us (1.12)
  blocking collectives: 300 us -> 358 us
    psum x1 -> x2, blocking collectives: 79.4 us -> 159 us  [body(): curvature = lax.psum(jnp.sum(direction * image_vec, axis=0), ('row', 'col'))]
    psum x2 -> x4, blocking collectives: 152 us -> 130 us  [the longest x2 71.8 us: squares(): lax.psum(lax.psum(jnp.sum(residual * residual, axis=0), 'col'), 'row')]
where the time goes in v1:
time: 615 us
  blocking collectives  358 us (58%)
  waiting for transfers between devices  182 us (30%)
  matrix products  51.2 us (8%)
  between operations  13.8 us (2%)
    psum x2, blocking collectives, body(): curvature = lax.psum(jnp.sum(direction * image_vec, axis=0), ('row', 'col'))  159 us
    reduce_scatter x2, waiting for transfers between devices, body(): lax.psum_scatter(kernel_product(row_points, col_points, col_values, kerne...  120 us
    psum x2, blocking collectives, squares(): lax.psum(lax.psum(jnp.sum(residual * residual, axis=0), 'col'), 'row')  71.8 us
    all_gather x2, waiting for transfers between devices, body(): col_values = lax.all_gather(direction, 'row', axis=0, tiled=True)  61 us
    psum x2, blocking collectives, squares(): lax.psum(jnp.sum(residual * residual, axis=0), 'col')  58.7 us
    dot_general x8, matrix products, apply_block(): jnp.dot(weights, values, preferred_element_type=jnp.float32, precision=la...  51.2 us
    all_gather x1, blocking collectives, body(): col_points = lax.all_gather(positions, 'row', axis=1, tiled=True)  40.7 us
    all_gather x1, blocking collectives, body(): row_points = lax.all_gather(positions, 'col', axis=1, tiled=True)  28 us
  transfers between devices with their start and end apart: 4, of which 3 were waited for; matrix products, arithmetic and copies ran while one was open for 0% of the time, Pallas kernels for 0%

profile of v1, /device:TPU:1, one launch (start us, length us, event | category | flops | bytes accessed | tf_op | source)
XLA Modules:
  0.0 614.7 jit_solution(5319018064573894291)
XLA Ops:
  7.2 0.7 all-gather.3.cloned.1.call-update
  7.9 40.7 %all_gather.13 = f32[3,2048]{1,0:T(4,128)S(1)} all-gather(f32[3,128]{1,0:T(4,128)} %param.7), channel_id=1, replica_groups=mesh['row'=16,'col'=16] {'row'}, dimensions={1}, use_global_device_ids=true | all-gather | bytes 26112 | tf_op jit(solution)/shard_map/all_gather | solution.py:46
  48.7 28.0 %all_gather.12 = f32[3,2048]{1,0:T(4,128)S(1)} all-gather(f32[3,128]{1,0:T(4,128)} %param.7), channel_id=1, replica_groups=mesh['row'=16,'col'=16] {'col'}, dimensions={1}, use_global_device_ids=true | all-gather | bytes 26112 | tf_op jit(solution)/shard_map/all_gather | solution.py:45
  76.6 0.2 broadcast.19.clone
  76.8 25.9 %while.20 = (s32[]{:T(128)}, f32[4,512,256]{2,1,0:T(8,128)S(1)}, f32[4,3,512]{2,1,0:T(4,128)S(1)}, f32[3,2048]{1,0:T(4,128)S(1)}, f32[2048,256]{1,0:T(8,128)}, /*index=5*/s32[]{:T(128)}, s32[]{:T(128)}, s32[]{}, s32[]{}) while((s32[]{:T(128)}, f32[4,512,256]{2,1,0:T(8,128)S(1)}, f32[4,3,512]{2,1,0:T(4,128)S(1)}, f32[3,2048]{1,0:T(4,128)S(1)}, ...), condition=%wide.region_4.5_spmd, body=%wide.region_3.4_spmd.sunk | while | flops 3231711232 | bytes 2713733 | solution.py:28
  76.8 6.4 %fusion.71 = f32[4,512,256]{2,1,0:T(8,128)S(1)} fusion(f32[4,512,256]{2,1,0:T(8,128)S(1)} %get-tuple-element.192, s32[]{:T(128)} %get-tuple-element.191, f32[2048,256]{1,0:T(8,128)} %get-tuple-element.204, f32[2048]{0:T(1024)S(1)} %bitcast.63, f32[512]{0:T(512)S(1)} %bitcast.70, f32[2048]{0:T(1024)S(1)} %bitcast.64, f32[512]{0:T(512)S(1)} %bitcast.69, ...), kind=kOutput, calls=%fused_computation.21.clone.1 | convolution fusion | flops 3231711232 | bytes 2652164 | tf_op jit(solution)/shard_map/while/body/eval_jaxpr/dot_general | solution.py:24
  83.3 6.4 %fusion.71 = f32[4,512,256]{2,1,0:T(8,128)S(1)} fusion(f32[4,512,256]{2,1,0:T(8,128)S(1)} %get-tuple-element.192, s32[]{:T(128)} %get-tuple-element.191, f32[2048,256]{1,0:T(8,128)} %get-tuple-element.204, f32[2048]{0:T(1024)S(1)} %bitcast.63, f32[512]{0:T(512)S(1)} %bitcast.70, f32[2048]{0:T(1024)S(1)} %bitcast.64, f32[512]{0:T(512)S(1)} %bitcast.69, ...), kind=kOutput, calls=%fused_computation.21.clone.1 | convolution fusion | flops 3231711232 | bytes 2652164 | tf_op jit(solution)/shard_map/while/body/eval_jaxpr/dot_general | solution.py:24
  89.8 6.4 %fusion.71 = f32[4,512,256]{2,1,0:T(8,128)S(1)} fusion(f32[4,512,256]{2,1,0:T(8,128)S(1)} %get-tuple-element.192, s32[]{:T(128)} %get-tuple-element.191, f32[2048,256]{1,0:T(8,128)} %get-tuple-element.204, f32[2048]{0:T(1024)S(1)} %bitcast.63, f32[512]{0:T(512)S(1)} %bitcast.70, f32[2048]{0:T(1024)S(1)} %bitcast.64, f32[512]{0:T(512)S(1)} %bitcast.69, ...), kind=kOutput, calls=%fused_computation.21.clone.1 | convolution fusion | flops 3231711232 | bytes 2652164 | tf_op jit(solution)/shard_map/while/body/eval_jaxpr/dot_general | solution.py:24
  96.3 6.4 %fusion.71 = f32[4,512,256]{2,1,0:T(8,128)S(1)} fusion(f32[4,512,256]{2,1,0:T(8,128)S(1)} %get-tuple-element.192, s32[]{:T(128)} %get-tuple-element.191, f32[2048,256]{1,0:T(8,128)} %get-tuple-element.204, f32[2048]{0:T(1024)S(1)} %bitcast.63, f32[512]{0:T(512)S(1)} %bitcast.70, f32[2048]{0:T(1024)S(1)} %bitcast.64, f32[512]{0:T(512)S(1)} %bitcast.69, ...), kind=kOutput, calls=%fused_computation.21.clone.1 | convolution fusion | flops 3231711232 | bytes 2652164 | tf_op jit(solution)/shard_map/while/body/eval_jaxpr/dot_general | solution.py:24
  102.7 1.3 copy-done.1
  104.1 58.5 %reduce-scatter.3.cloned.1.call-done = f32[128,256]{1,0:T(8,128)} async-done(((f32[2048,256]{1,0:T(8,128)}), f32[128,256]{1,0:T(8,128)}) %reduce-scatter.3.cloned.1.call-update) | async-done | bytes 131088 | tf_op jit(solution)/shard_map/reduce_scatter | solution.py:54
  162.6 1.0 multiply_reduce_fusion.2
  163.6 30.9 %psum.42 = f32[256]{0:T(256)S(1)} all-reduce(f32[256]{0:T(256)S(1)} %get-tuple-element.59), channel_id=1, replica_groups=mesh['row'=16,'col'=16] {'col'}, use_global_device_ids=true, to_apply=%region_1.0 | all-reduce | flops 256 | bytes 2048 | tf_op jit(solution)/shard_map/psum | solution.py:38
  194.5 37.1 %psum.43 = f32[256]{0:T(256)S(1)} all-reduce(f32[256]{0:T(256)S(1)} %psum.42), channel_id=1, replica_groups=mesh['row'=16,'col'=16] {'row'}, use_global_device_ids=true, to_apply=%region_2.0 | all-reduce | flops 256 | bytes 2048 | tf_op jit(solution)/shard_map/psum | solution.py:38
  231.6 79.6 %psum.44 = f32[256]{0:T(256)S(1)} all-reduce(f32[256]{0:T(256)S(1)} %get-tuple-element.58), channel_id=1, replica_groups=mesh['row'=16,'col'=16] {'row','col'}, use_global_device_ids=true, to_apply=%region_7.8 | all-reduce | flops 256 | bytes 2048 | tf_op jit(solution)/shard_map/psum | solution.py:61
  311.3 1.0 multiply_reduce_fusion.1
  312.3 27.8 %psum.45 = f32[256]{0:T(256)S(1)} all-reduce(f32[256]{0:T(256)S(1)} %get-tuple-element.80), channel_id=1, replica_groups=mesh['row'=16,'col'=16] {'col'}, use_global_device_ids=true, to_apply=%region_9.10 | all-reduce | flops 256 | bytes 2048 | tf_op jit(solution)/shard_map/psum | solution.py:38
  340.1 34.7 %psum.46 = f32[256]{0:T(256)S(1)} all-reduce(f32[256]{0:T(256)S(1)} %psum.45), channel_id=1, replica_groups=mesh['row'=16,'col'=16] {'row'}, use_global_device_ids=true, to_apply=%region_10.11 | all-reduce | flops 256 | bytes 2048 | tf_op jit(solution)/shard_map/psum | solution.py:38
  374.8 0.7 multiply_add_fusion.1
  375.5 0.2 reduce-scatter.5.cloned.1.call-start
  375.7 61.0 %all-gather.5.cloned.1.call-done = f32[2048,256]{1,0:T(8,128)} async-done(((f32[128,256]{1,0:T(8,128)}), f32[2048,256]{1,0:T(8,128)}) %all-gather.5.cloned.1.call-update) | async-done | bytes 2097168 | tf_op jit(solution)/shard_map/all_gather | solution.py:53
  436.7 0.2 broadcast.19
  436.9 25.9 %while.21 = (s32[]{:T(128)}, f32[4,512,256]{2,1,0:T(8,128)S(1)}, f32[4,3,512]{2,1,0:T(4,128)S(1)}, f32[3,2048]{1,0:T(4,128)S(1)}, f32[2048,256]{1,0:T(8,128)}, /*index=5*/s32[]{:T(128)}, s32[]{:T(128)}, s32[]{}, s32[]{}) while((s32[]{:T(128)}, f32[4,512,256]{2,1,0:T(8,128)S(1)}, f32[4,3,512]{2,1,0:T(4,128)S(1)}, f32[3,2048]{1,0:T(4,128)S(1)}, ...), condition=%wide.region_12.13_spmd, body=%wide.region_11.12_spmd.sunk | while | flops 3231711232 | bytes 2713733 | solution.py:28
  436.9 6.4 %fusion.75 = f32[4,512,256]{2,1,0:T(8,128)S(1)} fusion(f32[4,512,256]{2,1,0:T(8,128)S(1)} %get-tuple-element.219, s32[]{:T(128)} %get-tuple-element.218, f32[2048,256]{1,0:T(8,128)} %get-tuple-element.231, f32[2048]{0:T(1024)S(1)} %bitcast.66, f32[512]{0:T(512)S(1)} %bitcast.73, f32[2048]{0:T(1024)S(1)} %bitcast.67, f32[512]{0:T(512)S(1)} %bitcast.72, ...), kind=kOutput, calls=%fused_computation.48.clone.1 | convolution fusion | flops 3231711232 | bytes 2652164 | tf_op jit(solution)/shard_map/while/body/eval_jaxpr/dot_general | solution.py:24
  443.4 6.4 %fusion.75 = f32[4,512,256]{2,1,0:T(8,128)S(1)} fusion(f32[4,512,256]{2,1,0:T(8,128)S(1)} %get-tuple-element.219, s32[]{:T(128)} %get-tuple-element.218, f32[2048,256]{1,0:T(8,128)} %get-tuple-element.231, f32[2048]{0:T(1024)S(1)} %bitcast.66, f32[512]{0:T(512)S(1)} %bitcast.73, f32[2048]{0:T(1024)S(1)} %bitcast.67, f32[512]{0:T(512)S(1)} %bitcast.72, ...), kind=kOutput, calls=%fused_computation.48.clone.1 | convolution fusion | flops 3231711232 | bytes 2652164 | tf_op jit(solution)/shard_map/while/body/eval_jaxpr/dot_general | solution.py:24
  449.9 6.4 %fusion.75 = f32[4,512,256]{2,1,0:T(8,128)S(1)} fusion(f32[4,512,256]{2,1,0:T(8,128)S(1)} %get-tuple-element.219, s32[]{:T(128)} %get-tuple-element.218, f32[2048,256]{1,0:T(8,128)} %get-tuple-element.231, f32[2048]{0:T(1024)S(1)} %bitcast.66, f32[512]{0:T(512)S(1)} %bitcast.73, f32[2048]{0:T(1024)S(1)} %bitcast.67, f32[512]{0:T(512)S(1)} %bitcast.72, ...), kind=kOutput, calls=%fused_computation.48.clone.1 | convolution fusion | flops 3231711232 | bytes 2652164 | tf_op jit(solution)/shard_map/while/body/eval_jaxpr/dot_general | solution.py:24
  456.3 6.4 %fusion.75 = f32[4,512,256]{2,1,0:T(8,128)S(1)} fusion(f32[4,512,256]{2,1,0:T(8,128)S(1)} %get-tuple-element.219, s32[]{:T(128)} %get-tuple-element.218, f32[2048,256]{1,0:T(8,128)} %get-tuple-element.231, f32[2048]{0:T(1024)S(1)} %bitcast.66, f32[512]{0:T(512)S(1)} %bitcast.73, f32[2048]{0:T(1024)S(1)} %bitcast.67, f32[512]{0:T(512)S(1)} %bitcast.72, ...), kind=kOutput, calls=%fused_computation.48.clone.1 | convolution fusion | flops 3231711232 | bytes 2652164 | tf_op jit(solution)/shard_map/while/body/eval_jaxpr/dot_general | solution.py:24
  462.8 1.3 copy-done
  464.1 61.9 %reduce-scatter.5.cloned.1.call-done = f32[128,256]{1,0:T(8,128)} async-done(((f32[2048,256]{1,0:T(8,128)}), f32[128,256]{1,0:T(8,128)}) %reduce-scatter.5.cloned.1.call-update) | async-done | bytes 131088 | tf_op jit(solution)/shard_map/reduce_scatter | solution.py:54
  526.0 1.0 multiply_reduce_fusion
  527.0 79.5 %psum.47 = f32[256]{0:T(256)S(1)} all-reduce(f32[256]{0:T(256)S(1)} %multiply_reduce_fusion), channel_id=1, replica_groups=mesh['row'=16,'col'=16] {'row','col'}, use_global_device_ids=true, to_apply=%region_15.16 | all-reduce | flops 256 | bytes 2048 | tf_op jit(solution)/shard_map/psum | solution.py:61
  606.5 1.7 multiply_subtract_fusion
  (34 shorter events, 0.5 us)
Async XLA Ops:
  7.2 69.5 %all-gather.3.cloned.1.call-start = ((), (), s32[]{:S(2)}) async-start(), calls=%async_computation.2 | async-start | bytes 2228224 | tf_op jit(solution)/shard_map/all_gather | solution.py:53
  7.9 154.7 %reduce-scatter.3.cloned.1.call-start = ((), (), s32[]{:S(2)}) async-start(), calls=%async_computation.3 | async-start | bytes 2228224 | tf_op jit(solution)/shard_map/reduce_scatter | solution.py:54
  102.7 1.4 copy-start.1
  102.7 59.9 %copy-start.2 = (f32[128,256]{1,0:T(8,128)S(1)}, f32[128,256]{1,0:T(8,128)}, u32[]{:S(2)}) copy-start(f32[128,256]{1,0:T(8,128)} %param.9) | copy-start | bytes 393220
  102.7 59.9 %copy-start.4 = (f32[128]{0:T(128)S(1)}, f32[128]{0:T(128)}, u32[]{:S(2)}) copy-start(f32[128]{0:T(128)} %param.8) | copy-start | bytes 1540
  104.1 332.6 %all-gather.5.cloned.1.call-start = ((), (), s32[]{:S(2)}) async-start(), calls=%async_computation.4 | async-start | bytes 2228224 | tf_op jit(solution)/shard_map/all_gather | solution.py:53
  375.5 150.5 %reduce-scatter.5.cloned.1.call-start = ((), (), s32[]{:S(2)}) async-start(), calls=%async_computation.5 | async-start | bytes 2228224 | tf_op jit(solution)/shard_map/reduce_scatter | solution.py:54
  462.7 1.4 copy-start
  462.8 63.3 %copy-start.3 = (f32[128,256]{1,0:T(8,128)S(1)}, f32[128,256]{1,0:T(8,128)}, u32[]{:S(2)}) copy-start(f32[128,256]{1,0:T(8,128)} %multiply_add_fusion.1) | copy-start | bytes 393220
Sparse Core Ops, SparseCore 0:
  10.4 62.6 all-gather.2
  104.2 58.3 reduce-scatter.2
  375.6 61.0 all-gather.4
  464.2 61.7 reduce-scatter.4
